TPU v7x, 256 devices: a whole 4x4x8 slice. The times are simulated.
256 devices in a mesh: replica: 16 (over z, core), mp: 16 (over y, x).
Axes of the slice: x: 4, y: 4, z: 8, core: 2. Of those that a mesh axis runs over, the one named last changes fastest.
Arguments:
- gradients: bfloat16 [16, 8, 768, 3072], P('replica', None, 'mp'), may hold values from -6 to 6
- feedback: bfloat16 [16, 8, 768, 3072], P('replica', None, 'mp'), may hold values from -4 to 4
- right_init: bfloat16 [8, 3072, 32], replicated, may hold values from -0.109375 to 0.109375
- gram_root: float32 [8, 32, 32], replicated, as said below
- owners: int32 [8], replicated, may hold values from 0 to 15, as said below
- momentum: float32 [16, 1, 768, 3072], P('mp', None, 'replica'), may hold values from -4 to 4
- master_weights: float32 [16, 1, 768, 3072], P('mp', None, 'replica'), may hold values from -1.5 to 1.5
- vector_grads: float32 [16, 10752], P('replica', 'mp'), may hold values from -6 to 6
- vector_momentum: float32 [10752], P('mp'), may hold values from -6 to 6
- vector_params: float32 [10752], P('mp'), may hold values from -6 to 6
Outputs:
- new_feedback: bfloat16 [16, 8, 768, 3072], P('replica', None, 'mp')
- new_momentum: float32 [16, 1, 768, 3072], P('mp', None, 'replica')
- new_master: float32 [16, 1, 768, 3072], P('mp', None, 'replica')
- new_weights: bfloat16 [8, 768, 3072], P(None, 'replica')
- new_vector_momentum: float32 [10752], P('mp')
- new_vector_params: float32 [10752], P('mp')
Inputs may be any that keep to these rules, and one draw needn't show every extreme that they name: `owners`: every matrix has one owner; no owner holds more than 1 of the 8 matrices, and one owner holds exactly 1. `gram_root`: each matrix is the identity plus off-diagonal terms, times a positive scale.
All inputs are finite; a program needn't handle non-finite values.
Results may differ from a plain program's by a relative error of at most 0.007.
Values may be sent and summed in bfloat16 or wider, within the bound.
A program may use at most 192 MiB of HBM per device.

v0:
```python
import jax
import jax.numpy as jnp
from jax import lax
from jax.sharding import PartitionSpec as P


def per_device(
    gradients,
    feedback,
    right_init,
    gram_root,
    owners,
    momentum,
    master_weights,
    vector_grads,
    vector_momentum,
    vector_params,
):
    highest = lax.Precision.HIGHEST
    compensated = (gradients[0].astype(jnp.float32) + feedback[0].astype(jnp.float32)).astype(
        jnp.bfloat16
    )
    owner_count = lax.axis_size("mp")
    capacity = momentum.shape[1]
    matrices = owners.shape[0]
    replica_rows = momentum.shape[2]
    mp_index = lax.axis_index("mp")
    replica_index = lax.axis_index("replica")
    same_owner = owners[:, None] == owners[None, :]
    earlier = jnp.arange(matrices)[:, None] < jnp.arange(matrices)[None, :]
    ranks = jnp.sum((same_owner & earlier).astype(jnp.int32), axis=0)
    slots = owners * capacity + ranks
    slot_table = (slots[None, :] == jnp.arange(owner_count * capacity)[:, None]).astype(jnp.float32)
    table_narrow = slot_table.astype(jnp.bfloat16)
    table_mine = lax.dynamic_slice_in_dim(slot_table, mp_index * capacity, capacity, 0)
    left_terms = jnp.einsum(
        "kmn,knr->kmr", compensated, right_init, preferred_element_type=jnp.float32
    )
    left_sum = lax.psum(left_terms, "replica")
    left_rows = jnp.einsum("kmr,krs->kms", left_sum, gram_root, precision=highest).astype(
        jnp.bfloat16
    )
    right_terms = jnp.einsum(
        "kmn,kms->kns", compensated, left_rows, preferred_element_type=jnp.float32
    )
    right_new = lax.psum(right_terms, ("replica", "mp"))
    left_all = lax.all_gather(left_rows, "mp", axis=1, tiled=True)
    approx_rows = jnp.einsum(
        "kms,kns->kmn", left_rows.astype(jnp.float32), right_new, precision=highest
    )
    new_feedback = (compensated.astype(jnp.float32) - approx_rows).astype(jnp.bfloat16)
    left_chosen = jnp.einsum(
        "ck,kmr->cmr", table_mine.astype(jnp.bfloat16), left_all, preferred_element_type=jnp.float32
    )
    left_chosen = lax.dynamic_slice_in_dim(
        left_chosen, replica_index * replica_rows, replica_rows, 1
    )
    right_chosen = jnp.einsum("ck,knr->cnr", table_mine, right_new, precision=highest)
    approx_slots = jnp.einsum("cmr,cnr->cmn", left_chosen, right_chosen, precision=highest)
    new_momentum = 0.9 * momentum[0] + approx_slots
    new_master = master_weights[0] - 0.1 * new_momentum
    master_narrow = new_master.astype(jnp.bfloat16)
    weight_slots = lax.all_gather(master_narrow, "mp", axis=0, tiled=True)
    new_weights = jnp.einsum(
        "sk,smn->kmn", table_narrow, weight_slots, preferred_element_type=jnp.float32
    ).astype(jnp.bfloat16)
    vector_total = lax.psum(vector_grads[0], "replica")
    new_vector_momentum = 0.9 * vector_momentum + vector_total
    new_vector_params = vector_params - 0.1 * new_vector_momentum
    return (
        new_feedback[None],
        new_momentum[None],
        new_master[None],
        new_weights,
        new_vector_momentum,
        new_vector_params,
    )


def solution(mesh):
    return jax.shard_map(
        per_device,
        mesh=mesh,
        in_specs=(
            P("replica", None, "mp", None),
            P("replica", None, "mp", None),
            P(),
            P(),
            P(),
            P("mp", None, "replica", None),
            P("mp", None, "replica", None),
            P("replica", "mp"),
            P("mp"),
            P("mp"),
        ),
        out_specs=(
            P("replica", None, "mp", None),
            P("mp", None, "replica", None),
            P("mp", None, "replica", None),
            P(None, "replica", None),
            P("mp"),
            P("mp"),
        ),
        check_vma=False,
    )
```

profile of v0, /device:TPU:1, one launch (start us, length us, event | category | flops | bytes accessed | tf_op | source)
XLA Modules:
  0.0 481.2 jit_solution(16211220204946410669)
XLA Ops:
  7.2 0.0 copy-start
  7.2 0.0 all-reduce.3.cloned.1.call-start
  7.2 0.8 reduce.1
  8.0 0.6 copy-done
  8.6 3.1 fusion.27
  11.8 50.5 %all-reduce = (f32[8,48,32]{1,2,0:T(8,128)S(1)}, f32[672]{0:T(1024)S(1)}) all-reduce(f32[8,48,32]{1,2,0:T(8,128)S(1)} %fusion.27, f32[672]{0:T(1024)S(1)} %reduce.1), channel_id=1, replica_groups=mesh['replica'=16,'mp'=16] {'replica'}, use_global_device_ids=true, to_apply=%region_0.0 | all-reduce | flops 12960 | bytes 103680 | tf_op jit(solution)/shard_map/psum | solution.py:39
  62.2 0.0 copy-done.5
  62.3 0.4 convolution_convert_fusion
  62.6 4.7 fusion.25
  67.3 0.0 all-reduce.3.cloned.1.call-update
  67.4 0.0 all-gather.3.cloned.1.call-start
  67.4 0.1 copy.26
  67.6 0.4 copy-done.8
  68.0 0.1 convert_reduce_fusion
  68.1 22.7 %all_gather.6 = bf16[8,768,32]{2,0,1:T(8,128)(2,1)S(1)} all-gather(bf16[8,48,32]{2,0,1:T(8,128)(2,1)S(1)} %copy.26), channel_id=1, replica_groups=mesh['replica'=16,'mp'=16] {'mp'}, dimensions={1}, use_global_device_ids=true | all-gather | bytes 417792 | tf_op jit(solution)/shard_map/all_gather | solution.py:47
  90.8 1.1 multiply_reduce_fusion
  91.9 239.2 %all-reduce.3.cloned.1.call-done = f32[8,3072,32]{1,2,0:T(8,128)} async-done(((f32[8,3072,32]{1,2,0:T(8,128)}), f32[8,3072,32]{1,2,0:T(8,128)}) %all-reduce.3.cloned.1.call-update) | async-done | bytes 3145744 | tf_op jit(solution)/shard_map/psum | solution.py:46
  331.1 44.7 %fusion.6 = f32[1,3072,32]{0,1,2:T(8,128)} fusion(f32[8,3072,32]{1,2,0:T(8,128)} %all-reduce.3.cloned.1.call-done, pred[16,8]{1,0:T(8,128)(4,1)S(1)} %get-tuple-element.31, s32[]{:T(128)S(6)} %select_n.6), kind=kOutput, calls=%fused_computation.7 | convolution fusion | flops 9437184 | bytes 3539460 | tf_op jit(solution)/shard_map/ck,knr->cnr/dot_general | solution.py:58
  375.7 27.1 %copy.35 = f32[1,3072,32]{1,2,0:T(8,128)S(1)} copy(f32[1,3072,32]{0,1,2:T(8,128)} %fusion.6) | data formatting | bytes 786432 | tf_op jit(solution)/shard_map/ck,knr->cnr/dot_general | solution.py:58
  402.9 0.0 copy-start.6
  402.9 0.0 copy-start.7
  402.9 0.6 convolution_add_fusion
  403.6 0.0 copy-start.2
  403.6 1.2 fusion.10
  404.7 0.0 all-gather.3.cloned.1.call-update
  404.8 0.6 multiply_subtract_fusion
  405.4 7.4 %fusion.5 = bf16[1,8,48,3072]{3,2,1,0:T(8,128)(2,1)} fusion(bf16[8,48,32]{1,2,0:T(8,128)(2,1)S(1)} %convolution_convert_fusion, f32[8,3072,32]{1,2,0:T(8,128)} %all-reduce.3.cloned.1.call-done, bf16[1,8,48,3072]{3,2,1,0:T(8,128)(2,1)} %param.11, bf16[1,8,48,3072]{3,2,1,0:T(8,128)(2,1)} %param.10), kind=kOutput, calls=%fused_computation.5 | convolution fusion | flops 461242368 | bytes 10248192 | tf_op jit(solution)/shard_map/kms,kns->kmn/dot_general | solution.py:48
  412.8 0.0 copy-done.2
  412.8 51.4 %all-gather.3.cloned.1.call-done = bf16[768,3072]{1,0:T(8,128)(2,1)} async-done(((bf16[48,3072]{1,0:T(8,128)(2,1)}), bf16[768,3072]{1,0:T(8,128)(2,1)}) %all-gather.3.cloned.1.call-update) | async-done | bytes 4718608 | tf_op jit(solution)/shard_map/all_gather | solution.py:63
  464.2 7.5 %fusion.2 = bf16[8,48,3072]{2,0,1:T(8,128)(2,1)S(1)} fusion(bf16[16,48,3072]{2,1,0:T(8,128)(2,1)} %bitcast.41, s32[8]{0:T(128)S(1)} %add.27), kind=kOutput, calls=%fused_computation.4 | convolution fusion | flops 38928768 | bytes 7077920 | tf_op jit(solution)/shard_map/sk,smn->kmn/dot_general | solution.py:64
  471.7 2.7 copy.29
  474.4 0.0 copy-done.1
  (12 shorter events, 0.0 us)
Async XLA Ops:
  7.2 1.4 copy-start
  7.2 323.9 %all-reduce.3.cloned.1.call-start = ((), (), s32[]{:S(2)}) async-start(), calls=%async_computation | async-start | bytes 6291456 | tf_op jit(solution)/shard_map/psum | solution.py:46
  8.6 53.6 %copy-start.5 = (f32[8,32,32]{2,1,0:T(8,128)S(1)}, f32[8,32,32]{2,1,0:T(8,128)}, u32[]{:S(2)}) copy-start(f32[8,32,32]{2,1,0:T(8,128)} %param.13) | copy-start | bytes 98308
  67.3 0.7 copy-start.8
  67.4 396.9 %all-gather.3.cloned.1.call-start = ((), (), s32[]{:S(2)}) async-start(), calls=%async_computation.1 | async-start | bytes 5013504 | tf_op jit(solution)/shard_map/all_gather | solution.py:63
  375.7 27.1 %copy-start.3 = (f32[1,1,48,3072]{3,2,1,0:T(8,128)S(1)}, f32[1,1,48,3072]{3,2,1,0:T(8,128)}, u32[]{:S(2)}) copy-start(f32[1,1,48,3072]{3,2,1,0:T(8,128)} %param.15) | copy-start | bytes 1769476
  375.7 27.8 %copy-start.4 = (f32[1,1,48,3072]{3,2,1,0:T(8,128)S(1)}, f32[1,1,48,3072]{3,2,1,0:T(8,128)}, u32[]{:S(2)}) copy-start(f32[1,1,48,3072]{3,2,1,0:T(8,128)} %param.16) | copy-start | bytes 1769476
  402.9 1.9 copy-start.6
  402.9 1.9 copy-start.7
  403.6 9.2 %copy-start.2 = (f32[48,3072]{1,0:T(8,128)}, f32[48,3072]{1,0:T(8,128)S(1)}, u32[]{:S(2)}) copy-start(f32[48,3072]{1,0:T(8,128)S(1)} %convolution_add_fusion) | copy-start | bytes 1769476
  464.2 10.2 %copy-start.1 = (bf16[8,3072,32]{1,2,0:T(8,128)(2,1)S(1)}, bf16[8,3072,32]{1,2,0:T(8,128)(2,1)}, u32[]{:S(2)}) copy-start(bf16[8,3072,32]{1,2,0:T(8,128)(2,1)} %param.12) | copy-start | bytes 4718596
Sparse Core Ops, SparseCore 0:
  67.5 263.5 all-reduce.2
  404.9 59.2 all-gather.2
where the time goes:
time: 482 us; the launch traced here: 481 us
  waiting for transfers between devices  291 us (60%)
  blocking collectives  73.2 us (15%)
  matrix products  68.4 us (14%)
  local copies, waits for them, and re-layouts  31 us (6%)
  between operations  14.2 us (3%)
    psum x1, waiting for transfers between devices, per_device(): right_new = lax.psum(right_terms, ('replica', 'mp'))  239 us
    all_gather x1, waiting for transfers between devices, per_device(): weight_slots = lax.all_gather(master_narrow, 'mp', axis=0, tiled=True)  51.4 us
    psum x1, blocking collectives, per_device(): left_sum = lax.psum(left_terms, 'replica')  50.5 us
    dot_general x1, matrix products, per_device(): jnp.einsum('ck,knr->cnr', table_mine, right_new, precision=highest)  44.7 us
    dot_general x1, local copies, waits for them, and re-layouts, per_device(): jnp.einsum('ck,knr->cnr', table_mine, right_new, precision=highest)  27.1 us
    all_gather x1, blocking collectives, per_device(): left_all = lax.all_gather(left_rows, 'mp', axis=1, tiled=True)  22.7 us
  transfers between devices with their start and end apart: 2, of which 2 were waited for; matrix products, arithmetic and copies ran while one was open for 2% of the time, Pallas kernels for 0%

commit v1 on v0

--- a/solution.py
+++ b/solution.py
@@ -2,6 +2,22 @@
 import jax.numpy as jnp
 from jax import lax
 from jax.sharding import PartitionSpec as P
+
+
+def summed_both_ways(array, axis, dim, contribution):
+    size, here, span = (lax.axis_size(axis), lax.axis_index(axis), array.shape[dim])
+    ahead = [(i, (i + 1) % size) for i in range(size)]
+    left = [(i, (i - 1) % size) for i in range(size)]
+    half = size // 2
+    from_left = from_right = array
+    so_far = contribution(array, here * span)
+    for turn in range(1, half + 1):
+        from_left = lax.ppermute(from_left, axis, ahead)
+        if turn < size - half:
+            from_right = lax.ppermute(from_right, axis, left)
+            so_far = so_far + contribution(from_right, (here + turn) % size * span)
+        so_far = so_far + contribution(from_left, (here - turn) % size * span)
+    return so_far
 
 
 def per_device(
@@ -60,9 +76,16 @@
     new_momentum = 0.9 * momentum[0] + approx_slots
     new_master = master_weights[0] - 0.1 * new_momentum
     master_narrow = new_master.astype(jnp.bfloat16)
-    weight_slots = lax.all_gather(master_narrow, "mp", axis=0, tiled=True)
-    new_weights = jnp.einsum(
-        "sk,smn->kmn", table_narrow, weight_slots, preferred_element_type=jnp.float32
+    new_weights = summed_both_ways(
+        master_narrow,
+        "mp",
+        0,
+        lambda shard, offset: jnp.einsum(
+            "sk,smn->kmn",
+            lax.dynamic_slice_in_dim(table_narrow, offset, shard.shape[0], axis=0),
+            shard,
+            preferred_element_type=jnp.float32,
+        ),
     ).astype(jnp.bfloat16)
     vector_total = lax.psum(vector_grads[0], "replica")
     new_vector_momentum = 0.9 * vector_momentum + vector_total

time: 482 us -> 513 us (1.064); the launches traced: 481 us -> 505 us
  starting transfers between devices: 0.08 us -> 34.7 us
  waiting for transfers between devices: 291 us -> 282 us
  other arithmetic: 3.8 us -> 12.1 us
  matrix products: 68.4 us -> 60.2 us
    all_gather x1 -> x0, waiting for transfers between devices: 51.4 us -> none  [per_device(): weight_slots = lax.all_gather(master_narrow, 'mp', axis=0, tiled=True)]
    ppermute x0 -> x15, waiting for transfers between devices: none -> 44 us  [the longest x8 40.2 us: summed_both_ways(): from_left = lax.ppermute(from_left, axis, ahead)]
    ppermute x0 -> x15, starting transfers between devices: none -> 34.7 us  [the longest x7 33.4 us: summed_both_ways(): from_right = lax.ppermute(from_right, axis, left)]
    dot_general x1 -> x0, matrix products: 7.46 us -> none  [per_device(): jnp.einsum('sk,smn->kmn', table_narrow, weight_slots, preferred_element_t...]
    convert_element_type x2, other arithmetic: 1.17 us -> 7.69 us  [the longest x1 7.68 us: per_device(): new_weights = summed_both_ways(master_narrow, 'mp', 0, lambda shard, offs...]
  transfers between devices with their start and end apart: 2 -> 16, of which waited for: 2 -> 9; matrix products, arithmetic and copies ran while one was open for 2% -> 2% of each run, Pallas kernels for 0% -> 0%
where the time goes in v1:
time: 513 us; the launch traced here: 505 us
  waiting for transfers between devices  282 us (55%)
  blocking collectives  73.4 us (14%)
  matrix products  60.2 us (12%)
  starting transfers between devices  34.7 us (7%)
  local copies, waits for them, and re-layouts  27.9 us (5%)
  between operations  14.7 us (3%)
  other arithmetic  12.1 us (2%)
    psum x1, waiting for transfers between devices, per_device(): right_new = lax.psum(right_terms, ('replica', 'mp'))  238 us
    psum x1, blocking collectives, per_device(): left_sum = lax.psum(left_terms, 'replica')  50.5 us
    dot_general x1, matrix products, per_device(): jnp.einsum('ck,knr->cnr', table_mine, right_new, precision=highest)  44.6 us
    ppermute x8, waiting for transfers between devices, summed_both_ways(): from_left = lax.ppermute(from_left, axis, ahead)  40.2 us
    ppermute x7, starting transfers between devices, summed_both_ways(): from_right = lax.ppermute(from_right, axis, left)  33.4 us
    dot_general x1, local copies, waits for them, and re-layouts, per_device(): jnp.einsum('ck,knr->cnr', table_mine, right_new, precision=highest)  27.1 us
    all_gather x1, blocking collectives, per_device(): left_all = lax.all_gather(left_rows, 'mp', axis=1, tiled=True)  22.9 us
  transfers between devices with their start and end apart: 16, of which 9 were waited for; matrix products, arithmetic and copies ran while one was open for 2% of the time, Pallas kernels for 0%

profile of v1, /device:TPU:1, one launch (start us, length us, event | category | flops | bytes accessed | tf_op | source)
XLA Modules:
  0.0 505.3 jit_solution(5625127664454672344)
XLA Ops:
  7.2 0.8 reduce.1
  8.1 0.5 copy-done
  8.6 3.1 fusion.50
  11.7 50.5 %all-reduce = (f32[8,48,32]{1,2,0:T(8,128)S(1)}, f32[672]{0:T(1024)S(1)}) all-reduce(f32[8,48,32]{1,2,0:T(8,128)S(1)} %fusion.50, f32[672]{0:T(1024)S(1)} %reduce.1), channel_id=1, replica_groups=mesh['replica'=16,'mp'=16] {'replica'}, use_global_device_ids=true, to_apply=%region_0.0 | all-reduce | flops 12960 | bytes 103680 | tf_op jit(solution)/shard_map/psum | solution.py:55
  62.2 0.4 convolution_convert_fusion
  62.6 4.7 fusion.48
  67.9 22.9 %all_gather.3 = bf16[8,768,32]{2,0,1:T(8,128)(2,1)S(1)} all-gather(bf16[8,48,32]{2,0,1:T(8,128)(2,1)S(1)} %copy.20), channel_id=1, replica_groups=mesh['replica'=16,'mp'=16] {'mp'}, dimensions={1}, use_global_device_ids=true | all-gather | bytes 417792 | tf_op jit(solution)/shard_map/all_gather | solution.py:63
  90.9 1.1 multiply_reduce_fusion
  92.1 0.6 multiply_subtract_fusion
  92.7 238.4 %all-reduce.3.cloned.1.call-done = f32[8,3072,32]{1,2,0:T(8,128)} async-done(((f32[8,3072,32]{1,2,0:T(8,128)}), f32[8,3072,32]{1,2,0:T(8,128)}) %all-reduce.3.cloned.1.call-update) | async-done | bytes 3145744 | tf_op jit(solution)/shard_map/psum | solution.py:62
  331.0 44.6 %fusion.1 = f32[1,3072,32]{0,1,2:T(8,128)} fusion(f32[8,3072,32]{1,2,0:T(8,128)} %all-reduce.3.cloned.1.call-done, pred[16,8]{1,0:T(8,128)(4,1)S(1)} %get-tuple-element.31, s32[]{:T(128)S(6)} %select_n.115), kind=kOutput, calls=%fused_computation.5 | convolution fusion | flops 9437184 | bytes 3539460 | tf_op jit(solution)/shard_map/ck,knr->cnr/dot_general | solution.py:74
  375.7 27.1 %copy.26 = f32[1,3072,32]{1,2,0:T(8,128)S(1)} copy(f32[1,3072,32]{0,1,2:T(8,128)} %fusion.1) | data formatting | bytes 786432 | tf_op jit(solution)/shard_map/ck,knr->cnr/dot_general | solution.py:74
  402.8 0.6 convolution_add_fusion
  403.5 1.1 fusion.52
  404.6 1.2 collective-permute-start.1
  405.8 3.6 collective-permute-start
  409.4 6.7 %fusion = bf16[1,8,48,3072]{3,2,1,0:T(8,128)(2,1)} fusion(bf16[8,48,32]{1,2,0:T(8,128)(2,1)S(1)} %convolution_convert_fusion, f32[8,3072,32]{1,2,0:T(8,128)} %all-reduce.3.cloned.1.call-done, bf16[1,8,48,3072]{3,2,1,0:T(8,128)(2,1)S(1)} %copy-done.2, bf16[1,8,48,3072]{3,2,1,0:T(8,128)(2,1)} %param.10), kind=kOutput, calls=%fused_computation.3 | convolution fusion | flops 461242368 | bytes 10248192 | tf_op jit(solution)/shard_map/kms,kns->kmn/dot_general | solution.py:64
  416.2 4.8 collective-permute-start.2
  421.1 3.9 collective-permute-done.3
  425.1 4.9 collective-permute-start.4
  430.0 3.6 collective-permute-done.4
  433.6 5.2 %collective-permute-start.6 = (bf16[1,48,3072]{2,1,0:T(8,128)(2,1)S(1)}, bf16[1,48,3072]{2,1,0:T(8,128)(2,1)S(1)}, u32[]{:S(2)}, u32[]{:S(2)}) collective-permute-start(bf16[1,48,3072]{2,1,0:T(8,128)(2,1)S(1)} %collective-permute-done.4), channel_id=1, source_target_pairs={{0,15},{1,0},{2,1},{3,2},{4,3},{5,4},{6,5},{7,6},{8,7},{9,8},{10,9... | collective-permute-start | bytes 884744 | tf_op jit(solution)/shard_map/ppermute | solution.py:17
  439.0 8.8 %collective-permute-done.7 = bf16[1,48,3072]{2,1,0:T(8,128)(2,1)S(1)} collective-permute-done((bf16[1,48,3072]{2,1,0:T(8,128)(2,1)S(1)}, bf16[1,48,3072]{2,1,0:T(8,128)(2,1)S(1)}, u32[]{:S(2)}, u32[]{:S(2)}) %collective-permute-start.7) | collective-permute-done | bytes 294944 | tf_op jit(solution)/shard_map/ppermute | solution.py:15
  447.9 4.9 collective-permute-start.8
  452.8 4.3 collective-permute-done.9
  457.1 4.9 collective-permute-start.10
  462.1 5.4 %collective-permute-done.11 = bf16[1,48,3072]{2,1,0:T(8,128)(2,1)S(1)} collective-permute-done((bf16[1,48,3072]{2,1,0:T(8,128)(2,1)S(1)}, bf16[1,48,3072]{2,1,0:T(8,128)(2,1)S(1)}, u32[]{:S(2)}, u32[]{:S(2)}) %collective-permute-start.11) | collective-permute-done | bytes 294944 | tf_op jit(solution)/shard_map/ppermute | solution.py:15
  467.5 5.1 %collective-permute-start.12 = (bf16[1,48,3072]{2,1,0:T(8,128)(2,1)S(1)}, bf16[1,48,3072]{2,1,0:T(8,128)(2,1)S(1)}, u32[]{:S(2)}, u32[]{:S(2)}) collective-permute-start(bf16[1,48,3072]{2,1,0:T(8,128)(2,1)S(1)} %collective-permute-done.10), channel_id=1, source_target_pairs={{0,15},{1,0},{2,1},{3,2},{4,3},{5,4},{6,5},{7,6},{8,7},{9,8},{10,9... | collective-permute-start | bytes 884744 | tf_op jit(solution)/shard_map/ppermute | solution.py:17
  472.7 6.2 %collective-permute-done.13 = bf16[1,48,3072]{2,1,0:T(8,128)(2,1)S(1)} collective-permute-done((bf16[1,48,3072]{2,1,0:T(8,128)(2,1)S(1)}, bf16[1,48,3072]{2,1,0:T(8,128)(2,1)S(1)}, u32[]{:S(2)}, u32[]{:S(2)}) %collective-permute-start.13) | collective-permute-done | bytes 294944 | tf_op jit(solution)/shard_map/ppermute | solution.py:15
  478.9 0.2 collective-permute-done.12
  479.1 11.6 %collective-permute-done.14 = bf16[1,48,3072]{2,1,0:T(8,128)(2,1)S(1)} collective-permute-done((bf16[1,48,3072]{2,1,0:T(8,128)(2,1)S(1)}, bf16[1,48,3072]{2,1,0:T(8,128)(2,1)S(1)}, u32[]{:S(2)}, u32[]{:S(2)}) %collective-permute-start.14) | collective-permute-done | bytes 294944 | tf_op jit(solution)/shard_map/ppermute | solution.py:15
  490.8 7.7 %add_convert_fusion = bf16[8,48,3072]{2,1,0:T(8,128)(2,1)} fusion(f32[48,3072]{1,0:T(8,128)S(1)} %bitcast_convert_fusion, f32[8]{0:T(128)S(1)} %get-tuple-element.14, f32[48,3072]{1,0:T(8,128)S(1)} %bitcast_convert_fusion.1, f32[8]{0:T(128)S(1)} %get-tuple-element.15, f32[48,3072]{1,0:T(8,128)S(1)} %bitcast_convert_fusion.2, f32[8]{0:T(128)S(1)} %get-tuple-element.16, ...), kind=kLoop, calls=%fused_computation | loop fusion | flops 37748736 | bytes 11796992 | tf_op jit(solution)/shard_map/convert_element_type | solution.py:89
  (56 shorter events, 1.2 us)
Async XLA Ops:
  7.2 1.4 copy-start
  7.2 55.0 %copy-start.6 = (f32[8,32,32]{2,1,0:T(8,128)S(1)}, f32[8,32,32]{2,1,0:T(8,128)}, u32[]{:S(2)}) copy-start(f32[8,32,32]{2,1,0:T(8,128)} %param.13) | copy-start | bytes 98308
  7.2 323.9 %all-reduce.3.cloned.1.call-start = ((), (), s32[]{:S(2)}) async-start(), calls=%async_computation | async-start | bytes 6291456 | tf_op jit(solution)/shard_map/psum | solution.py:62
  62.6 5.1 %copy-start.9 = (s32[8]{0:T(128)S(1)}, s32[8]{0:T(128)}, u32[]{:S(2)}) copy-start(s32[8]{0:T(128)} %param.14) | copy-start | bytes 100
  67.3 24.7 %copy-start.7 = (f32[672]{0:T(1024)S(1)}, f32[672]{0:T(1024)}, u32[]{:S(2)}) copy-start(f32[672]{0:T(1024)} %param.19) | copy-start | bytes 8068
  67.3 24.7 %copy-start.8 = (f32[672]{0:T(1024)S(1)}, f32[672]{0:T(1024)}, u32[]{:S(2)}) copy-start(f32[672]{0:T(1024)} %param.18) | copy-start | bytes 8068
  375.7 27.1 %copy-start.4 = (f32[1,1,48,3072]{3,2,1,0:T(8,128)S(1)}, f32[1,1,48,3072]{3,2,1,0:T(8,128)}, u32[]{:S(2)}) copy-start(f32[1,1,48,3072]{3,2,1,0:T(8,128)} %param.15) | copy-start | bytes 1769476
  375.7 27.8 %copy-start.5 = (f32[1,1,48,3072]{3,2,1,0:T(8,128)S(1)}, f32[1,1,48,3072]{3,2,1,0:T(8,128)}, u32[]{:S(2)}) copy-start(f32[1,1,48,3072]{3,2,1,0:T(8,128)} %param.16) | copy-start | bytes 1769476
  402.8 6.6 %copy-start.2 = (bf16[1,8,48,3072]{3,2,1,0:T(8,128)(2,1)S(1)}, bf16[1,8,48,3072]{3,2,1,0:T(8,128)(2,1)}, u32[]{:S(2)}) copy-start(bf16[1,8,48,3072]{3,2,1,0:T(8,128)(2,1)} %param.11) | copy-start | bytes 7077892
  403.5 12.6 %copy-start.3 = (f32[48,3072]{1,0:T(8,128)}, f32[48,3072]{1,0:T(8,128)S(1)}, u32[]{:S(2)}) copy-start(f32[48,3072]{1,0:T(8,128)S(1)} %convolution_add_fusion) | copy-start | bytes 1769476
  404.6 11.5 %collective-permute-start.1 = (bf16[1,48,3072]{2,1,0:T(8,128)(2,1)S(1)}, bf16[1,48,3072]{2,1,0:T(8,128)(2,1)S(1)}, u32[]{:S(2)}, u32[]{:S(2)}) collective-permute-start(bf16[1,48,3072]{2,1,0:T(8,128)(2,1)S(1)} %bitcast.165), channel_id=1, source_target_pairs={{0,1},{1,2},{2,3},{3,4},{4,5},{5,6},{6,7},{7,8},{8,9},{9,10},{10,1... | collective-permute-start | bytes 884744 | tf_op jit(solution)/shard_map/ppermute | solution.py:15
  405.8 10.4 %collective-permute-start = (bf16[1,48,3072]{2,1,0:T(8,128)(2,1)S(1)}, bf16[1,48,3072]{2,1,0:T(8,128)(2,1)S(1)}, u32[]{:S(2)}, u32[]{:S(2)}) collective-permute-start(bf16[1,48,3072]{2,1,0:T(8,128)(2,1)S(1)} %bitcast.166), channel_id=1, source_target_pairs={{0,15},{1,0},{2,1},{3,2},{4,3},{5,4},{6,5},{7,6},{8,7},{9,8},{10,9... | collective-permute-start | bytes 884744 | tf_op jit(solution)/shard_map/ppermute | solution.py:17
  416.1 8.9 %collective-permute-start.3 = (bf16[1,48,3072]{2,1,0:T(8,128)(2,1)S(1)}, bf16[1,48,3072]{2,1,0:T(8,128)(2,1)S(1)}, u32[]{:S(2)}, u32[]{:S(2)}) collective-permute-start(bf16[1,48,3072]{2,1,0:T(8,128)(2,1)S(1)} %collective-permute-done.1), channel_id=1, source_target_pairs={{0,1},{1,2},{2,3},{3,4},{4,5},{5,6},{6,7},{7,8},{8,9},{9,10},{10,1... | collective-permute-start | bytes 884744 | tf_op jit(solution)/shard_map/ppermute | solution.py:15
  416.2 8.9 %collective-permute-start.2 = (bf16[1,48,3072]{2,1,0:T(8,128)(2,1)S(1)}, bf16[1,48,3072]{2,1,0:T(8,128)(2,1)S(1)}, u32[]{:S(2)}, u32[]{:S(2)}) collective-permute-start(bf16[1,48,3072]{2,1,0:T(8,128)(2,1)S(1)} %collective-permute-done), channel_id=1, source_target_pairs={{0,15},{1,0},{2,1},{3,2},{4,3},{5,4},{6,5},{7,6},{8,7},{9,8},{10,9... | collective-permute-start | bytes 884744 | tf_op jit(solution)/shard_map/ppermute | solution.py:17
  425.0 13.9 %collective-permute-start.5 = (bf16[1,48,3072]{2,1,0:T(8,128)(2,1)S(1)}, bf16[1,48,3072]{2,1,0:T(8,128)(2,1)S(1)}, u32[]{:S(2)}, u32[]{:S(2)}) collective-permute-start(bf16[1,48,3072]{2,1,0:T(8,128)(2,1)S(1)} %collective-permute-done.3), channel_id=1, source_target_pairs={{0,1},{1,2},{2,3},{3,4},{4,5},{5,6},{6,7},{7,8},{8,9},{9,10},{10,1... | collective-permute-start | bytes 884744 | tf_op jit(solution)/shard_map/ppermute | solution.py:15
  425.1 8.5 %collective-permute-start.4 = (bf16[1,48,3072]{2,1,0:T(8,128)(2,1)S(1)}, bf16[1,48,3072]{2,1,0:T(8,128)(2,1)S(1)}, u32[]{:S(2)}, u32[]{:S(2)}) collective-permute-start(bf16[1,48,3072]{2,1,0:T(8,128)(2,1)S(1)} %collective-permute-done.2), channel_id=1, source_target_pairs={{0,15},{1,0},{2,1},{3,2},{4,3},{5,4},{6,5},{7,6},{8,7},{9,8},{10,9... | collective-permute-start | bytes 884744 | tf_op jit(solution)/shard_map/ppermute | solution.py:17
  433.6 14.3 %collective-permute-start.6 = (bf16[1,48,3072]{2,1,0:T(8,128)(2,1)S(1)}, bf16[1,48,3072]{2,1,0:T(8,128)(2,1)S(1)}, u32[]{:S(2)}, u32[]{:S(2)}) collective-permute-start(bf16[1,48,3072]{2,1,0:T(8,128)(2,1)S(1)} %collective-permute-done.4), channel_id=1, source_target_pairs={{0,15},{1,0},{2,1},{3,2},{4,3},{5,4},{6,5},{7,6},{8,7},{9,8},{10,9... | collective-permute-start | bytes 884744 | tf_op jit(solution)/shard_map/ppermute | solution.py:17
  438.9 9.0 %collective-permute-start.7 = (bf16[1,48,3072]{2,1,0:T(8,128)(2,1)S(1)}, bf16[1,48,3072]{2,1,0:T(8,128)(2,1)S(1)}, u32[]{:S(2)}, u32[]{:S(2)}) collective-permute-start(bf16[1,48,3072]{2,1,0:T(8,128)(2,1)S(1)} %collective-permute-done.5), channel_id=1, source_target_pairs={{0,1},{1,2},{2,3},{3,4},{4,5},{5,6},{6,7},{7,8},{8,9},{9,10},{10,1... | collective-permute-start | bytes 884744 | tf_op jit(solution)/shard_map/ppermute | solution.py:15
  447.8 9.2 %collective-permute-start.9 = (bf16[1,48,3072]{2,1,0:T(8,128)(2,1)S(1)}, bf16[1,48,3072]{2,1,0:T(8,128)(2,1)S(1)}, u32[]{:S(2)}, u32[]{:S(2)}) collective-permute-start(bf16[1,48,3072]{2,1,0:T(8,128)(2,1)S(1)} %collective-permute-done.7), channel_id=1, source_target_pairs={{0,1},{1,2},{2,3},{3,4},{4,5},{5,6},{6,7},{7,8},{8,9},{9,10},{10,1... | collective-permute-start | bytes 884744 | tf_op jit(solution)/shard_map/ppermute | solution.py:15
  447.9 9.2 %collective-permute-start.8 = (bf16[1,48,3072]{2,1,0:T(8,128)(2,1)S(1)}, bf16[1,48,3072]{2,1,0:T(8,128)(2,1)S(1)}, u32[]{:S(2)}, u32[]{:S(2)}) collective-permute-start(bf16[1,48,3072]{2,1,0:T(8,128)(2,1)S(1)} %collective-permute-done.6), channel_id=1, source_target_pairs={{0,15},{1,0},{2,1},{3,2},{4,3},{5,4},{6,5},{7,6},{8,7},{9,8},{10,9... | collective-permute-start | bytes 884744 | tf_op jit(solution)/shard_map/ppermute | solution.py:17
  457.1 10.3 %collective-permute-start.11 = (bf16[1,48,3072]{2,1,0:T(8,128)(2,1)S(1)}, bf16[1,48,3072]{2,1,0:T(8,128)(2,1)S(1)}, u32[]{:S(2)}, u32[]{:S(2)}) collective-permute-start(bf16[1,48,3072]{2,1,0:T(8,128)(2,1)S(1)} %collective-permute-done.9), channel_id=1, source_target_pairs={{0,1},{1,2},{2,3},{3,4},{4,5},{5,6},{6,7},{7,8},{8,9},{9,10},{10,1... | collective-permute-start | bytes 884744 | tf_op jit(solution)/shard_map/ppermute | solution.py:15
  457.1 10.3 %collective-permute-start.10 = (bf16[1,48,3072]{2,1,0:T(8,128)(2,1)S(1)}, bf16[1,48,3072]{2,1,0:T(8,128)(2,1)S(1)}, u32[]{:S(2)}, u32[]{:S(2)}) collective-permute-start(bf16[1,48,3072]{2,1,0:T(8,128)(2,1)S(1)} %collective-permute-done.8), channel_id=1, source_target_pairs={{0,15},{1,0},{2,1},{3,2},{4,3},{5,4},{6,5},{7,6},{8,7},{9,8},{10,9... | collective-permute-start | bytes 884744 | tf_op jit(solution)/shard_map/ppermute | solution.py:17
  467.4 11.4 %collective-permute-start.13 = (bf16[1,48,3072]{2,1,0:T(8,128)(2,1)S(1)}, bf16[1,48,3072]{2,1,0:T(8,128)(2,1)S(1)}, u32[]{:S(2)}, u32[]{:S(2)}) collective-permute-start(bf16[1,48,3072]{2,1,0:T(8,128)(2,1)S(1)} %collective-permute-done.11), channel_id=1, source_target_pairs={{0,1},{1,2},{2,3},{3,4},{4,5},{5,6},{6,7},{7,8},{8,9},{9,10},{10,1... | collective-permute-start | bytes 884744 | tf_op jit(solution)/shard_map/ppermute | solution.py:15
  467.5 11.6 %collective-permute-start.12 = (bf16[1,48,3072]{2,1,0:T(8,128)(2,1)S(1)}, bf16[1,48,3072]{2,1,0:T(8,128)(2,1)S(1)}, u32[]{:S(2)}, u32[]{:S(2)}) collective-permute-start(bf16[1,48,3072]{2,1,0:T(8,128)(2,1)S(1)} %collective-permute-done.10), channel_id=1, source_target_pairs={{0,15},{1,0},{2,1},{3,2},{4,3},{5,4},{6,5},{7,6},{8,7},{9,8},{10,9... | collective-permute-start | bytes 884744 | tf_op jit(solution)/shard_map/ppermute | solution.py:17
  478.8 11.9 %collective-permute-start.14 = (bf16[1,48,3072]{2,1,0:T(8,128)(2,1)S(1)}, bf16[1,48,3072]{2,1,0:T(8,128)(2,1)S(1)}, u32[]{:S(2)}, u32[]{:S(2)}) collective-permute-start(bf16[1,48,3072]{2,1,0:T(8,128)(2,1)S(1)} %collective-permute-done.13), channel_id=1, source_target_pairs={{0,1},{1,2},{2,3},{3,4},{4,5},{5,6},{6,7},{7,8},{8,9},{9,10},{10,1... | collective-permute-start | bytes 884744 | tf_op jit(solution)/shard_map/ppermute | solution.py:15
  490.8 7.7 %copy-start.1 = (bf16[8,3072,32]{1,2,0:T(8,128)(2,1)S(1)}, bf16[8,3072,32]{1,2,0:T(8,128)(2,1)}, u32[]{:S(2)}) copy-start(bf16[8,3072,32]{1,2,0:T(8,128)(2,1)} %param.12) | copy-start | bytes 4718596
Sparse Core Ops, SparseCore 0:
  67.5 263.5 all-reduce.2
